TPU v7x, 32 devices: a whole 2x2x4 slice. The times are simulated.
32 devices in a mesh: row: 4 (over y, x), col: 8 (over z, core).
Axes of the slice: x: 2, y: 2, z: 4, core: 2. Of those that a mesh axis runs over, the one named last changes fastest.
Arguments:
- trail: float32 [2, 4, 512, 2, 8, 512], P(None, 'row', None, None, 'col'), may hold values from -6 to 6
- panel: float32 [2, 4, 512, 512], P(None, 'row', None, 'col'), may hold values from -6 to 6
- row_basis: float32 [2, 4, 64, 512], P(None, 'row', None, 'col'), may hold values from -0.75 to 0.75
- row_coeff: float32 [2, 4, 64, 512], P(None, 'row', None, 'col'), may hold values from -0.25 to 0.25
- col_basis: float32 [2, 8, 64, 512], P(None, 'col', None, 'row'), may hold values from -0.75 to 0.75
- col_scaled: float32 [2, 8, 64, 512], P(None, 'col', None, 'row'), may hold values from -0.25 to 0.25
- pivot_basis: float32 [64, 512], P(None, 'col'), may hold values from -0.75 to 0.75
- pivot_scaled: float32 [64, 512], replicated, may hold values from -0.25 to 0.25
- sketch: float32 [64, 512], replicated, may hold values from -6 to 6
- perm: int32 [512], replicated, may hold values from 0 to 511, each once
- pair_kind: int32 [256], replicated, may hold values from 0 to 1
- pivot_values: float32 [3, 256], replicated, may hold values from -3 to 3, as said below
Outputs:
- trail_out: float32 [2, 4, 512, 2, 8, 512], P(None, 'row', None, None, 'col')
- basis_out: float32 [2, 4, 64, 512], P(None, 'row')
- coeff_out: float32 [2, 4, 64, 512], P(None, 'row')
Inputs may be any that keep to these rules, and one draw needn't show every extreme that they name: `pivot_values`: rows 0 and 1 have magnitudes between 0.5 and 0.7; row 2 has magnitude 1.2 or more.
All inputs are finite; a program needn't handle non-finite values.
Results may differ from a plain program's by a relative error of at most 0.00013.
Values sent between devices are 32-bit elements; how exact they have to be, the bound alone decides.
No kernel may reach another device: no remote copies, remote signals or barrier semaphores. Data moves between devices by JAX's collectives and lax.ppermute only.
A program may use at most 64 MiB of HBM per device.

v0:
```python
import jax
import jax.numpy as jnp
from jax import lax
from jax.sharding import PartitionSpec as P


def pair_apply(rows, pair_kind, pivot_values):
    shaped = rows.reshape(rows.shape[:-1] + (rows.shape[-1] // 2, 2))
    first_in = shaped[..., 0]
    second_in = shaped[..., 1]
    diag_one = pivot_values[0]
    diag_two = pivot_values[1]
    offdiag = pivot_values[2]
    determinant = diag_one * diag_two - offdiag * offdiag
    twin = pair_kind == 1
    first = jnp.where(
        twin, (first_in * diag_two - second_in * offdiag) / determinant, first_in / diag_one
    )
    second = jnp.where(
        twin, (second_in * diag_one - first_in * offdiag) / determinant, second_in / diag_two
    )
    return jnp.stack([first, second], axis=-1).reshape(rows.shape)


def tri_solve(lower, rhs):
    return jax.vmap(lambda low, right: jax.scipy.linalg.solve_triangular(low, right, lower=True))(
        lower, rhs
    )


def body(
    trail,
    panel,
    row_basis,
    row_coeff,
    col_basis,
    col_scaled,
    pivot_basis,
    pivot_scaled,
    sketch,
    perm,
    pair_kind,
    pivot_values,
):
    highest = lax.Precision.HIGHEST
    width = sketch.shape[1]
    block = panel.shape[3]
    xrows, yrows = (
        lax.all_gather(row_basis, "col", axis=3, tiled=True),
        lax.all_gather(row_coeff, "col", axis=3, tiled=True),
    )
    zcols, gcols = (
        lax.all_gather(col_basis, "row", axis=3, tiled=True),
        lax.all_gather(col_scaled, "row", axis=3, tiled=True),
    )
    xrows = xrows[:, 0]
    yrows = yrows[:, 0]
    zcols = zcols[:, 0]
    gcols = gcols[:, 0]
    core = jnp.einsum("arp,bsp->arbs", yrows, gcols, precision=highest)
    left = jnp.einsum("arp,arbs->apbs", xrows, core, precision=highest)
    change = jnp.einsum("apbs,bsq->apbq", left, zcols, precision=highest)
    trail_out = trail - change[:, None, :, :, None, :]
    pcore = jnp.einsum("arp,sp->ars", yrows, pivot_scaled, precision=highest)
    pleft = jnp.einsum("arp,ars->aps", xrows, pcore, precision=highest)
    updated = panel[:, 0] - jnp.einsum("aps,sq->apq", pleft, pivot_basis, precision=highest)
    scaled_t = pair_apply(sketch, pair_kind, pivot_values)
    column_ids = lax.axis_index("col") * block + jnp.arange(block, dtype=jnp.int32)
    selector = (perm[:, None] == column_ids[None, :]).astype(jnp.float32)
    local_sketch = jnp.dot(scaled_t, selector, precision=highest)
    partial_range = jnp.einsum("apq,rq->arp", updated, local_sketch, precision=highest)
    range_t = lax.psum(partial_range, "col")
    gram = jnp.einsum("arp,asp->ars", range_t, range_t, precision=highest) / width
    basis = tri_solve(jnp.linalg.cholesky(gram), range_t)
    projected_part = jnp.einsum("arp,apq->arq", basis, updated, precision=highest)
    projected = lax.all_gather(projected_part, "col", axis=2, tiled=True)
    permuted = jnp.take(projected, perm, axis=2)
    coeff = pair_apply(permuted, pair_kind, pivot_values) / jnp.sqrt(jnp.float32(width))
    return (trail_out, basis[:, None], coeff[:, None])


def solution(mesh):
    return jax.shard_map(
        body,
        mesh=mesh,
        in_specs=(
            P(None, "row", None, None, "col", None),
            P(None, "row", None, "col"),
            P(None, "row", None, "col"),
            P(None, "row", None, "col"),
            P(None, "col", None, "row"),
            P(None, "col", None, "row"),
            P(None, "col"),
            P(),
            P(),
            P(),
            P(),
            P(),
        ),
        out_specs=(
            P(None, "row", None, None, "col", None),
            P(None, "row", None, None),
            P(None, "row", None, None),
        ),
        check_vma=False,
    )
```

profile of v0, /device:TPU:0, one launch (start us, length us, event | category | flops | bytes accessed | tf_op | source)
XLA Modules:
  0.0 159.1 jit_solution(12313392400558865005)
XLA Ops:
  7.3 0.8 broadcast_compare_fusion
  8.1 0.8 fusion.16
  8.9 0.9 copy.54
  9.8 0.9 copy.51
  10.8 1.0 copy.59
  11.8 16.5 %all_gather.15 = f32[2,1,64,512]{2,0,1,3:T(2,128)S(1)} all-gather(f32[2,1,64,64]{2,0,1,3:T(2,128)S(1)} %copy.51), channel_id=1, replica_groups=mesh['row'=4,'col'=8] {'col'}, dimensions={3}, use_global_device_ids=true | all-gather | bytes 294912 | tf_op jit(solution)/shard_map/all_gather | solution.py:50
  28.5 14.8 %all_gather.17 = f32[2,1,64,512]{2,0,1,3:T(2,128)S(1)} all-gather(f32[2,1,64,64]{2,0,1,3:T(2,128)S(1)} %copy.54), channel_id=1, replica_groups=mesh['row'=4,'col'=8] {'col'}, dimensions={3}, use_global_device_ids=true | all-gather | bytes 294912 | tf_op jit(solution)/shard_map/all_gather | solution.py:49
  43.5 2.2 %broadcast_select_fusion.4 = (f32[64,256,1]{0,2,1:T(1,128)S(1)}, f32[64,256,1]{0,2,1:T(1,128)S(1)}) fusion(pred[256]{0:T(512)(128)(4,1)S(1)} %broadcast_compare_fusion, f32[64,256,2]{0,2,1:T(2,128)S(1)} %bitcast.82, f32[256]{0:T(256)S(1)} %bitcast.90, f32[256]{0:T(256)S(1)} %bitcast.96, f32[256]{0:T(256)S(1)} %bitcast.93, f32[256]{0:T(256)S(1)} %bitcast.87), kind=kLoop, calls=%fused_computation.21 | loop fusion | flops 196608 | bytes 266496 | tf_op jit(solution)/shard_map/jit(_where)/select_n | solution.py:16
  45.7 0.3 pad_maximum_fusion
  46.0 0.5 fusion.6
  46.5 0.4 convolution_bitcast_fusion.2
  46.8 0.5 convolution_bitcast_fusion.3
  47.3 0.4 convolution_subtract_fusion
  47.7 1.1 convolution_bitcast_fusion.1
  48.9 10.3 %all_gather.18 = f32[2,1,64,512]{3,2,0,1:T(8,128)S(1)} all-gather(f32[2,1,64,128]{3,2,0,1:T(8,128)S(1)} %bitcast.85), channel_id=1, replica_groups=mesh['row'=4,'col'=8] {'row'}, dimensions={3}, use_global_device_ids=true | all-gather | bytes 327680 | tf_op jit(solution)/shard_map/all_gather | solution.py:53
  59.2 10.2 %all_gather.16 = f32[2,1,64,512]{3,2,0,1:T(8,128)S(1)} all-gather(f32[2,1,64,128]{3,2,0,1:T(8,128)S(1)} %bitcast.86), channel_id=1, replica_groups=mesh['row'=4,'col'=8] {'row'}, dimensions={3}, use_global_device_ids=true | all-gather | bytes 327680 | tf_op jit(solution)/shard_map/all_gather | solution.py:54
  69.4 0.5 fusion.1
  69.9 0.6 convolution_bitcast_fusion
  70.5 7.2 %bitcast_subtract_fusion = f32[2,1,512,2,1,512]{5,2,0,3,4,1:T(8,128)} fusion(f32[2,1,512,2,1,512]{5,4,3,2,1,0:T(1,128)} %param.12, f32[2,512,2,64]{1,3,0,2:T(8,128)S(1)} %convolution_bitcast_fusion, f32[2,1,64,512]{3,2,0,1:T(8,128)S(1)} %all_gather.18), kind=kOutput, calls=%fused_computation.1 | convolution fusion | flops 806354944 | bytes 9175040 | tf_op jit(solution)/shard_map/apbs,bsq->apbq/dot_general | solution.py:62
  77.9 8.5 %copy.66 = f32[2,1,512,2,1,512]{5,4,3,2,1,0:T(1,128)} copy(f32[2,1,512,2,1,512]{5,2,0,3,4,1:T(8,128)} %bitcast_subtract_fusion) | data formatting | bytes 8388608
  86.4 19.4 %all-reduce.2.cloned.1.call-done = f32[2,64,512]{2,1,0:T(8,128)} async-done(((f32[2,64,512]{2,1,0:T(8,128)}), f32[2,64,512]{2,1,0:T(8,128)}) %all-reduce.2.cloned.1.call-update) | async-done | bytes 262160 | tf_op jit(solution)/shard_map/psum | solution.py:72
  105.8 1.4 fusion.17
  107.3 11.7 %custom-call.8 = f32[2,64,64]{2,1,0:T(8,128)S(1)} custom-call(f32[2,64,64]{2,1,0:T(8,128)S(1)} %fusion.14), custom_call_target="Cholesky" | custom-call | tf_op jit(solution)/shard_map/jit(cholesky)/cholesky | solution.py:74
  119.3 9.8 %custom-call.9 = f32[2,1,64,64]{2,3,1,0:T(8,128)S(1)} custom-call(f32[2,1,64,64]{3,2,1,0:T(8,128)S(1)} %select_bitcast_fusion), custom_call_target="InvertDiagBlocksLowerTriangular" | custom-call | tf_op jit(solution)/shard_map/vmap(jit(_solve_triangular))/triangular_solve | solution.py:26
  129.1 1.4 fusion.12
  130.5 0.4 fusion.18
  131.0 15.1 %all_gather.19 = f32[2,64,512]{1,0,2:T(2,128)S(1)} all-gather(f32[2,64,64]{1,0,2:T(2,128)S(1)} %copy.64), channel_id=1, replica_groups=mesh['row'=4,'col'=8] {'col'}, dimensions={2}, use_global_device_ids=true | all-gather | bytes 294912 | tf_op jit(solution)/shard_map/all_gather | solution.py:76
  146.1 2.1 %gather_fusion = f32[512,2,64]{2,1,0:T(2,128)S(1)} fusion(f32[2,64,512]{1,0,2:T(2,128)S(1)} %all_gather.19, s32[1024]{0:T(1024)S(1)} %pad_clamp_fusion), kind=kCustom, calls=%fused_computation | custom fusion | bytes 526336 | tf_op jit(solution)/shard_map/jit(_take)/gather | solution.py:77
  148.2 0.4 broadcast_select_fusion.2
  148.6 2.2 %broadcast_select_fusion.1 = (f32[2,64,256,1]{1,3,2,0:T(1,128)S(1)}, f32[2,64,256,1]{1,3,2,0:T(1,128)S(1)}) fusion(pred[256]{0:T(512)(128)(4,1)S(1)} %broadcast_compare_fusion, f32[2,64,256,2]{1,3,2,0:T(2,128)S(1)} %broadcast_select_fusion.2, f32[256]{0:T(256)S(1)} %bitcast.92, f32[256]{0:T(256)S(1)} %multiply_subtract_fusion, f32[256]{0:T(256)S(1)} %bitcast.95, ...), kind=kLoop, calls=%fused_computation.9 | loop fusion | flops 393216 | bytes 528640 | tf_op jit(solution)/shard_map/jit(_where)/select_n | solution.py:16
  150.8 0.6 maximum_multiply_fusion
  151.4 0.9 copy.68
  (33 shorter events, 1.1 us)
Async XLA Ops:
  7.2 38.8 %copy-start = (f32[64,512]{1,0:T(8,128)S(1)}, f32[64,512]{1,0:T(8,128)}, u32[]{:S(2)}) copy-start(f32[64,512]{1,0:T(8,128)} %param.19) | copy-start | bytes 393220
  7.2 39.7 %copy-start.6 = (s32[512]{0:T(512)S(1)}, s32[512]{0:T(512)}, u32[]{:S(2)}) copy-start(s32[512]{0:T(512)} %param.21) | copy-start | bytes 6148
  7.2 40.1 %copy-start.5 = (f32[64,64]{1,0:T(8,128)S(1)}, f32[64,64]{1,0:T(8,128)}, u32[]{:S(2)}) copy-start(f32[64,64]{1,0:T(8,128)} %param.18) | copy-start | bytes 49156
  7.2 40.1 %copy-start.2 = (f32[2,1,512,64]{2,3,1,0:T(8,128)S(1)}, f32[2,1,512,64]{2,3,1,0:T(8,128)}, u32[]{:S(2)}) copy-start(f32[2,1,512,64]{2,3,1,0:T(8,128)} %param.13) | copy-start | bytes 786436
  7.2 41.7 %copy-start.3 = (f32[2,1,64,128]{3,2,1,0:T(8,128)S(1)}, f32[2,1,64,128]{3,2,1,0:T(8,128)}, u32[]{:S(2)}) copy-start(f32[2,1,64,128]{3,2,1,0:T(8,128)} %param.16) | copy-start | bytes 196612
  7.2 52.0 %copy-start.4 = (f32[2,1,64,128]{3,2,1,0:T(8,128)S(1)}, f32[2,1,64,128]{3,2,1,0:T(8,128)}, u32[]{:S(2)}) copy-start(f32[2,1,64,128]{3,2,1,0:T(8,128)} %param.17) | copy-start | bytes 196612
  7.2 98.6 %all-reduce.2.cloned.1.call-start = ((), (), s32[]{:S(2)}) async-start(), calls=%async_computation | async-start | bytes 524288 | tf_op jit(solution)/shard_map/psum | solution.py:72
  130.5 21.8 %copy-start.1 = (f32[2,64,512]{2,1,0:T(8,128)}, f32[2,64,512]{2,1,0:T(8,128)S(1)}, u32[]{:S(2)}) copy-start(f32[2,64,512]{2,1,0:T(8,128)S(1)} %fusion.12) | copy-start | bytes 786436
Sparse Core Ops, SparseCore 0:
  49.0 56.7 all-reduce.1
where the time goes:
time: 160 us; the launch traced here: 159 us
  blocking collectives  66.8 us (42%)
  other arithmetic  29.1 us (18%)
  waiting for transfers between devices  19.4 us (12%)
  local copies, waits for them, and re-layouts  15.2 us (10%)
  between operations  14.4 us (9%)
  matrix products  14.3 us (9%)
    psum x1, waiting for transfers between devices, body(): range_t = lax.psum(partial_range, 'col')  19.4 us
    all_gather x1, blocking collectives, body(): lax.all_gather(row_coeff, 'col', axis=3, tiled=True)  16.5 us
    all_gather x1, blocking collectives, body(): projected = lax.all_gather(projected_part, 'col', axis=2, tiled=True)  15.1 us
    all_gather x1, blocking collectives, body(): lax.all_gather(row_basis, 'col', axis=3, tiled=True)  14.8 us
    unnamed x19, local copies, waits for them, and re-layouts  12.3 us
    another operation x4, other arithmetic, body(): basis = tri_solve(jnp.linalg.cholesky(gram), range_t)  11.9 us
    all_gather x1, blocking collectives, body(): lax.all_gather(col_basis, 'row', axis=3, tiled=True)  10.3 us
    all_gather x1, blocking collectives, body(): lax.all_gather(col_scaled, 'row', axis=3, tiled=True)  10.2 us
  transfers between devices with their start and end apart: 1, of which 1 were waited for; matrix products, arithmetic and copies ran while one was open for 11% of the time, Pallas kernels for 0%

commit v1 on v0

--- a/solution.py
+++ b/solution.py
@@ -69,7 +69,8 @@
     selector = (perm[:, None] == column_ids[None, :]).astype(jnp.float32)
     local_sketch = jnp.dot(scaled_t, selector, precision=highest)
     partial_range = jnp.einsum("apq,rq->arp", updated, local_sketch, precision=highest)
-    range_t = lax.psum(partial_range, "col")
+    blocks = lax.all_gather(partial_range, "col")
+    range_t = jnp.sum(blocks, axis=0)
     gram = jnp.einsum("arp,asp->ars", range_t, range_t, precision=highest) / width
     basis = tri_solve(jnp.linalg.cholesky(gram), range_t)
     projected_part = jnp.einsum("arp,apq->arq", basis, updated, precision=highest)

time: 160 us -> 137 us (0.86)
  waiting for transfers between devices: 19.4 us -> 0.04 us
  matrix products: 14.3 us -> 11 us
  local copies, waits for them, and re-layouts: 15.2 us -> 13 us
  other arithmetic: 29.1 us -> 30.9 us
    psum x1 -> x0, waiting for transfers between devices: 19.4 us -> none  [body(): range_t = lax.psum(partial_range, 'col')]
    unnamed x19, local copies, waits for them, and re-layouts: 12.3 us -> 10.1 us
    reduce_sum x0 -> x1, other arithmetic: none -> 1.82 us  [body(): range_t = jnp.sum(blocks, axis=0)]
  transfers between devices with their start and end apart: 1 -> 1, of which waited for: 1 -> 0; matrix products, arithmetic and copies ran while one was open for 11% -> 10% of each run, Pallas kernels for 0% -> 0%
where the time goes in v1:
time: 137 us
  blocking collectives  67.3 us (49%)
  other arithmetic  30.9 us (23%)
  between operations  14.4 us (11%)
  local copies, waits for them, and re-layouts  13 us (9%)
  matrix products  11 us (8%)
    all_gather x1, blocking collectives, body(): lax.all_gather(row_coeff, 'col', axis=3, tiled=True)  16.5 us
    all_gather x1, blocking collectives, body(): projected = lax.all_gather(projected_part, 'col', axis=2, tiled=True)  15.5 us
    all_gather x1, blocking collectives, body(): lax.all_gather(row_basis, 'col', axis=3, tiled=True)  14.8 us
    another operation x4, other arithmetic, body(): basis = tri_solve(jnp.linalg.cholesky(gram), range_t)  11.9 us
    all_gather x1, blocking collectives, body(): lax.all_gather(col_basis, 'row', axis=3, tiled=True)  10.3 us
    all_gather x1, blocking collectives, body(): lax.all_gather(col_scaled, 'row', axis=3, tiled=True)  10.2 us
    unnamed x19, local copies, waits for them, and re-layouts  10.1 us
    another operation x3, other arithmetic, tri_solve(): jax.scipy.linalg.solve_triangular(low, right, lower=True)  9.92 us
  transfers between devices with their start and end apart: 1, of which 0 were waited for; matrix products, arithmetic and copies ran while one was open for 10% of the time, Pallas kernels for 0%

profile of v1, /device:TPU:0, one launch (start us, length us, event | category | flops | bytes accessed | tf_op | source)
XLA Modules:
  0.0 136.7 jit_solution(2824210151659662704)
XLA Ops:
  7.3 0.8 broadcast_compare_fusion
  8.1 0.8 fusion.16
  8.9 0.9 copy.54
  9.8 0.9 copy.51
  10.8 1.0 copy.59
  11.8 16.5 %all_gather.21 = f32[2,1,64,512]{2,0,1,3:T(2,128)S(1)} all-gather(f32[2,1,64,64]{2,0,1,3:T(2,128)S(1)} %copy.51), channel_id=1, replica_groups=mesh['row'=4,'col'=8] {'col'}, dimensions={3}, use_global_device_ids=true | all-gather | bytes 294912 | tf_op jit(solution)/shard_map/all_gather | solution.py:50
  28.5 14.8 %all_gather.23 = f32[2,1,64,512]{2,0,1,3:T(2,128)S(1)} all-gather(f32[2,1,64,64]{2,0,1,3:T(2,128)S(1)} %copy.54), channel_id=1, replica_groups=mesh['row'=4,'col'=8] {'col'}, dimensions={3}, use_global_device_ids=true | all-gather | bytes 294912 | tf_op jit(solution)/shard_map/all_gather | solution.py:49
  43.5 2.2 %broadcast_select_fusion.4 = (f32[64,256,1]{0,2,1:T(1,128)S(1)}, f32[64,256,1]{0,2,1:T(1,128)S(1)}) fusion(pred[256]{0:T(512)(128)(4,1)S(1)} %broadcast_compare_fusion, f32[64,256,2]{0,2,1:T(2,128)S(1)} %bitcast.84, f32[256]{0:T(256)S(1)} %bitcast.92, f32[256]{0:T(256)S(1)} %bitcast.98, f32[256]{0:T(256)S(1)} %bitcast.95, f32[256]{0:T(256)S(1)} %bitcast.89), kind=kLoop, calls=%fused_computation.21 | loop fusion | flops 196608 | bytes 266496 | tf_op jit(solution)/shard_map/jit(_where)/select_n | solution.py:16
  45.7 0.3 pad_maximum_fusion
  46.0 0.5 fusion.6
  46.5 0.4 convolution_bitcast_fusion.2
  46.9 0.5 convolution_bitcast_fusion.3
  47.3 0.4 convolution_subtract_fusion
  47.8 1.1 convolution_bitcast_fusion.1
  49.0 10.3 %all_gather.24 = f32[2,1,64,512]{3,2,0,1:T(8,128)S(1)} all-gather(f32[2,1,64,128]{3,2,0,1:T(8,128)S(1)} %bitcast.87), channel_id=1, replica_groups=mesh['row'=4,'col'=8] {'row'}, dimensions={3}, use_global_device_ids=true | all-gather | bytes 327680 | tf_op jit(solution)/shard_map/all_gather | solution.py:53
  59.4 10.2 %all_gather.22 = f32[2,1,64,512]{3,2,0,1:T(8,128)S(1)} all-gather(f32[2,1,64,128]{3,2,0,1:T(8,128)S(1)} %bitcast.88), channel_id=1, replica_groups=mesh['row'=4,'col'=8] {'row'}, dimensions={3}, use_global_device_ids=true | all-gather | bytes 327680 | tf_op jit(solution)/shard_map/all_gather | solution.py:54
  69.5 0.5 fusion.1
  70.1 0.6 convolution_bitcast_fusion
  70.6 6.0 %bitcast_subtract_fusion = f32[2,1,512,2,1,512]{5,2,0,3,4,1:T(8,128)S(1)} fusion(f32[2,1,512,2,1,512]{5,4,3,2,1,0:T(1,128)} %param.12, f32[2,512,2,64]{1,3,0,2:T(8,128)S(1)} %convolution_bitcast_fusion, f32[2,1,64,512]{3,2,0,1:T(8,128)S(1)} %all_gather.24), kind=kOutput, calls=%fused_computation.1 | convolution fusion | flops 806354944 | bytes 9175040 | tf_op jit(solution)/shard_map/apbs,bsq->apbq/dot_general | solution.py:62
  76.6 6.3 %copy.66 = f32[2,1,512,2,1,512]{5,4,3,2,1,0:T(1,128)} copy(f32[2,1,512,2,1,512]{5,2,0,3,4,1:T(8,128)S(1)} %bitcast_subtract_fusion) | data formatting | bytes 8388608
  83.0 1.8 %reduce_sum.9 = f32[2,64,512]{2,1,0:T(8,128)S(1)} reduce(f32[8,2,64,512]{3,2,1,0:T(8,128)} %bitcast.80, f32[]{:T(128)} %constant.67.clone.1), dimensions={0}, to_apply=%region_0.1 | reduce | flops 458752 | bytes 2359300 | tf_op jit(solution)/shard_map/reduce_sum | solution.py:73
  84.9 0.4 fusion.17
  85.3 11.7 %custom-call.8 = f32[2,64,64]{2,1,0:T(8,128)S(1)} custom-call(f32[2,64,64]{2,1,0:T(8,128)S(1)} %fusion.14), custom_call_target="Cholesky" | custom-call | tf_op jit(solution)/shard_map/jit(cholesky)/cholesky | solution.py:75
  97.3 9.8 %custom-call.9 = f32[2,1,64,64]{2,3,1,0:T(8,128)S(1)} custom-call(f32[2,1,64,64]{3,2,1,0:T(8,128)S(1)} %select_bitcast_fusion), custom_call_target="InvertDiagBlocksLowerTriangular" | custom-call | tf_op jit(solution)/shard_map/vmap(jit(_solve_triangular))/triangular_solve | solution.py:26
  107.1 0.4 fusion.12
  107.6 0.4 fusion.18
  108.0 15.5 %all_gather.27 = f32[2,64,512]{1,0,2:T(2,128)S(1)} all-gather(f32[2,64,64]{1,0,2:T(2,128)S(1)} %copy.64), channel_id=1, replica_groups=mesh['row'=4,'col'=8] {'col'}, dimensions={2}, use_global_device_ids=true | all-gather | bytes 294912 | tf_op jit(solution)/shard_map/all_gather | solution.py:77
  123.6 2.1 %gather_fusion = f32[512,2,64]{2,1,0:T(2,128)S(1)} fusion(f32[2,64,512]{1,0,2:T(2,128)S(1)} %all_gather.27, s32[1024]{0:T(1024)S(1)} %pad_clamp_fusion), kind=kCustom, calls=%fused_computation | custom fusion | bytes 526336 | tf_op jit(solution)/shard_map/jit(_take)/gather | solution.py:78
  125.7 0.4 broadcast_select_fusion.2
  126.1 2.2 %broadcast_select_fusion.1 = (f32[2,64,256,1]{1,3,2,0:T(1,128)S(1)}, f32[2,64,256,1]{1,3,2,0:T(1,128)S(1)}) fusion(pred[256]{0:T(512)(128)(4,1)S(1)} %broadcast_compare_fusion, f32[2,64,256,2]{1,3,2,0:T(2,128)S(1)} %broadcast_select_fusion.2, f32[256]{0:T(256)S(1)} %bitcast.94, f32[256]{0:T(256)S(1)} %multiply_subtract_fusion, f32[256]{0:T(256)S(1)} %bitcast.97, ...), kind=kLoop, calls=%fused_computation.9 | loop fusion | flops 393216 | bytes 528640 | tf_op jit(solution)/shard_map/jit(_where)/select_n | solution.py:16
  128.3 0.6 maximum_multiply_fusion
  128.9 0.9 copy.68
  (34 shorter events, 1.2 us)
Async XLA Ops:
  7.2 38.8 %copy-start = (f32[64,512]{1,0:T(8,128)S(1)}, f32[64,512]{1,0:T(8,128)}, u32[]{:S(2)}) copy-start(f32[64,512]{1,0:T(8,128)} %param.19) | copy-start | bytes 393220
  7.2 39.7 %copy-start.6 = (s32[512]{0:T(512)S(1)}, s32[512]{0:T(512)}, u32[]{:S(2)}) copy-start(s32[512]{0:T(512)} %param.21) | copy-start | bytes 6148
  7.2 40.1 %copy-start.5 = (f32[64,64]{1,0:T(8,128)S(1)}, f32[64,64]{1,0:T(8,128)}, u32[]{:S(2)}) copy-start(f32[64,64]{1,0:T(8,128)} %param.18) | copy-start | bytes 49156
  7.2 40.1 %copy-start.2 = (f32[2,1,512,64]{2,3,1,0:T(8,128)S(1)}, f32[2,1,512,64]{2,3,1,0:T(8,128)}, u32[]{:S(2)}) copy-start(f32[2,1,512,64]{2,3,1,0:T(8,128)} %param.13) | copy-start | bytes 786436
  7.2 41.8 %copy-start.3 = (f32[2,1,64,128]{3,2,1,0:T(8,128)S(1)}, f32[2,1,64,128]{3,2,1,0:T(8,128)}, u32[]{:S(2)}) copy-start(f32[2,1,64,128]{3,2,1,0:T(8,128)} %param.16) | copy-start | bytes 196612
  7.2 52.2 %copy-start.4 = (f32[2,1,64,128]{3,2,1,0:T(8,128)S(1)}, f32[2,1,64,128]{3,2,1,0:T(8,128)}, u32[]{:S(2)}) copy-start(f32[2,1,64,128]{3,2,1,0:T(8,128)} %param.17) | copy-start | bytes 196612
  7.2 75.8 %all-gather.3.cloned.1.call-start = ((), (), s32[]{:S(2)}) async-start(), calls=%async_computation | async-start | bytes 2359296 | tf_op jit(solution)/shard_map/all_gather | solution.py:72
  107.6 22.3 %copy-start.1 = (f32[2,64,512]{2,1,0:T(8,128)}, f32[2,64,512]{2,1,0:T(8,128)S(1)}, u32[]{:S(2)}) copy-start(f32[2,64,512]{2,1,0:T(8,128)S(1)} %fusion.12) | copy-start | bytes 786436
Sparse Core Ops, SparseCore 0:
  49.0 30.5 all-gather.2
